TPU v7x, 32 devices: a whole 2x2x4 slice. The times are simulated.
32 devices in a mesh: groups: 2 (over y), seq: 16 (over z, x, core).
Axes of the slice: x: 2, y: 2, z: 4, core: 2. Of those that a mesh axis runs over, the one named last changes fastest.
Arguments:
- key_values: bfloat16 [3, 2048, 8192], P(None, 'seq', 'groups'), parts along dimension 2, may hold values from -14 to 14, as said below
- bases: bfloat16 [3, 2, 1024, 256], replicated, may hold values from -0.1875 to 0.1875
- owner_slots: int32 [3, 64], P(None, ('groups', 'seq')), parts along dimension 1, may hold values from 0 to 15, as said below
Outputs:
- received: bfloat16 [512, 512, 128], P(('groups', 'seq')), parts along dimension 0
- grams: float32 [6, 2, 256, 256], P('groups'), parts along dimension 0
- energies: float32 [6, 2, 1024], P('groups'), parts along dimension 0
There are 2 independent parts, one for each index of `groups`. A program takes and returns all parts, laid end to end along the dimension named above; an argument that names none is the same for every part. Nothing has to cross between parts.
Inputs may be any that keep to these rules, and one draw needn't show every extreme that they name: key_values are finite real values within the range. `owner_slots`: block j of a layer belongs to device j // 2 of seq; the 6 values of one device's blocks over all layers are distinct, so an owner's slot is written at most once; some owner has all 16 slots filled.
All inputs are finite; a program needn't handle non-finite values.
Results may differ from a plain program's by a relative error of at most 0.001.
Values may be sent and summed in bfloat16 or wider, within the bound.
A program may use at most 128 MiB of HBM per device.

v0:
```python
import jax
import jax.numpy as jnp
from jax import lax
from jax.sharding import PartitionSpec as P

REACH = 8
OWNER_SLOT_LIMIT = 2
CAP = 16


def from_behind(block, axis, distance):
    devices = range(lax.axis_size(axis))
    route = [((i - distance) % len(devices), i) for i in devices]
    return lax.ppermute(block, axis, route)


def per_device(key_values, bases, owner_slots):
    dev_count = lax.axis_size("seq")
    layers = key_values.shape[0]
    width = bases.shape[2]
    rank = bases.shape[3]
    tok_dev = key_values.shape[2] // dev_count
    tokens = tok_dev * dev_count
    blk_dev = owner_slots.shape[1]
    blk_rows = tok_dev // blk_dev
    whole = lax.all_to_all(key_values, "seq", split_axis=2, concat_axis=1, tiled=True)
    gram_list = []
    energy_list = []
    block_list = []
    for layer_idx in range(layers):
        slab_rows = whole[layer_idx]
        slab_rows = slab_rows.reshape(2, width, tok_dev)
        basis = bases[layer_idx]
        coeff = jnp.einsum(
            "scr,sct->srt", basis, slab_rows, preferred_element_type=jnp.float32
        ).astype(jnp.bfloat16)
        recon = jnp.einsum("scr,srt->sct", basis, coeff, preferred_element_type=jnp.float32)
        resid = slab_rows.astype(jnp.float32) - recon
        energy_term = jnp.sum(resid * resid, axis=2)
        gram_term = jnp.einsum("srt,sqt->srq", coeff, coeff, preferred_element_type=jnp.float32)
        gram_total, energy_total = lax.psum((gram_term, energy_term), "seq")
        gram_list.append(gram_total / tokens)
        energy_list.append(energy_total / tokens)
        block_list.append(coeff.reshape(2 * rank, blk_dev, blk_rows).transpose(1, 0, 2))
    grams = jnp.stack(gram_list)
    energies = jnp.stack(energy_list)
    unit_count = layers * blk_dev
    units = jnp.stack(block_list).reshape(unit_count, 2 * rank * blk_rows)
    slot_vals = owner_slots.reshape(unit_count)
    one_hot = (slot_vals[:, None] == jnp.arange(CAP, dtype=jnp.int32)[None, :]).astype(jnp.bfloat16)
    outgoing = jnp.einsum("us,uf->sf", one_hot, units, preferred_element_type=jnp.float32).astype(
        jnp.bfloat16
    )
    outgoing = outgoing.reshape(REACH, OWNER_SLOT_LIMIT, 2 * rank, blk_rows)
    arrived = [outgoing[0]]
    for offset in range(1, REACH):
        arrived.append(from_behind(outgoing[offset], "seq", offset))
    buffer_all = jnp.stack(arrived)
    received = buffer_all.reshape(REACH * OWNER_SLOT_LIMIT, 2 * rank, blk_rows)
    return (received, grams, energies)


def solution(mesh):
    in_specs = (P(None, "seq", "groups"), P(), P(None, ("groups", "seq")))
    out_specs = (
        P(("groups", "seq"), None, None),
        P("groups", None, None, None),
        P("groups", None, None),
    )
    return jax.shard_map(
        per_device, mesh=mesh, in_specs=in_specs, out_specs=out_specs, check_vma=False
    )
```

profile of v0, /device:TPU:1, one launch (start us, length us, event | category | flops | bytes accessed | tf_op | source)
XLA Modules:
  0.0 328.1 jit_solution(11468838820563559150)
XLA Ops:
  7.2 7.2 %copy.39 = bf16[3,128,4096]{1,0,2:T(4,128)(2,1)} copy(bf16[3,128,4096]{2,1,0:T(8,128)(2,1)} %param.3) | data formatting | bytes 6291456 | tf_op args[0]
  14.4 7.5 %all-to-all-start = ((bf16[3,128,4096]{1,0,2:T(4,128)(2,1)}), bf16[3,128,4096]{1,0,2:T(4,128)(2,1)}, u32[]{:S(2)}, u32[]{:S(2)}) async-start(bf16[3,128,4096]{1,0,2:T(4,128)(2,1)} %copy.39), calls=%async_computation | async-start | bytes 8388608 | tf_op jit(solution)/shard_map/all_to_all | solution.py:26
  22.1 77.9 %all-to-all-done = bf16[3,128,4096]{1,0,2:T(4,128)(2,1)} async-done(((bf16[3,128,4096]{1,0,2:T(4,128)(2,1)}), bf16[3,128,4096]{1,0,2:T(4,128)(2,1)}, u32[]{:S(2)}, u32[]{:S(2)}) %all-to-all-start) | async-done | bytes 3145760 | tf_op jit(solution)/shard_map/all_to_all | solution.py:26
  100.0 5.5 %copy.40 = bf16[3,128,16,256]{3,1,2,0:T(8,128)(2,1)S(1)} copy(bf16[3,128,16,256]{1,0,3,2:T(4,128)(2,1)} %bitcast.1) | data formatting | bytes 6291456 | tf_op jit(solution)/shard_map/all_to_all | solution.py:26
  105.5 1.6 fusion.21
  107.1 1.0 copy-done.4
  109.9 1.8 convolution_convert_fusion.1
  111.6 1.9 fusion.1
  113.6 1.7 convolution_convert_fusion.3
  115.4 1.8 fusion.5
  117.2 1.1 fusion.22
  118.3 1.1 fusion.23
  119.3 1.1 fusion.24
  120.6 0.9 convolution_convert_fusion
  121.5 1.5 slice_bitcast_fusion
  123.1 0.7 bitcast_dynamic-update-slice_fusion
  123.8 5.6 %collective-permute-start = (bf16[2,512,128]{2,1,0:T(8,128)(2,1)S(1)}, bf16[2,512,128]{2,1,0:T(8,128)(2,1)S(1)}, u32[]{:S(2)}, u32[]{:S(2)}) collective-permute-start(bf16[2,512,128]{2,1,0:T(8,128)(2,1)S(1)} %bitcast.154), channel_id=1, source_target_pairs={{15,0},{0,1},{1,2},{2,3},{3,4},{4,5},{5,6},{6,7},{7,8},{8,9},{9,10... | collective-permute-start | bytes 786440 | tf_op jit(solution)/shard_map/ppermute | solution.py:14
  129.5 10.1 %collective-permute-start.1 = (bf16[2,512,128]{2,1,0:T(8,128)(2,1)S(1)}, bf16[2,512,128]{2,1,0:T(8,128)(2,1)S(1)}, u32[]{:S(2)}, u32[]{:S(2)}) collective-permute-start(bf16[2,512,128]{2,1,0:T(8,128)(2,1)S(1)} %bitcast.153), channel_id=1, source_target_pairs={{14,0},{15,1},{0,2},{1,3},{2,4},{3,5},{4,6},{5,7},{6,8},{7,9},{8,1... | collective-permute-start | bytes 786440 | tf_op jit(solution)/shard_map/ppermute | solution.py:14
  139.6 2.1 collective-permute-start.2
  141.7 1.1 collective-permute-start.3
  142.8 1.4 collective-permute-start.4
  144.2 69.8 %all-reduce = (f32[2,1024]{1,0:T(2,128)S(1)}, f32[2,1024]{1,0:T(2,128)S(1)}, f32[2,1024]{1,0:T(2,128)S(1)}) all-reduce(f32[2,1024]{1,0:T(2,128)S(1)} %fusion.1, f32[2,1024]{1,0:T(2,128)S(1)} %fusion.3, f32[2,1024]{1,0:T(2,128)S(1)} %fusion.5), channel_id=1, replica_groups=mesh['groups'=2,'seq'=16] {'seq'}, use_global_device_ids=true, to_apply=%region_8.0 | all-reduce | flops 6144 | bytes 49152 | tf_op jit(solution)/shard_map/psum | solution.py:41
  214.9 0.7 bitcast_dynamic-update-slice_fusion.7
  215.6 2.2 collective-permute-start.6
  218.6 0.7 bitcast_dynamic-update-slice_fusion.5
  220.0 0.7 bitcast_dynamic-update-slice_fusion.3
  220.7 18.3 %collective-permute-done.5 = bf16[2,512,128]{2,1,0:T(8,128)(2,1)S(1)} collective-permute-done((bf16[2,512,128]{2,1,0:T(8,128)(2,1)S(1)}, bf16[2,512,128]{2,1,0:T(8,128)(2,1)S(1)}, u32[]{:S(2)}, u32[]{:S(2)}) %collective-permute-start.5) | collective-permute-done | bytes 262176 | tf_op jit(solution)/shard_map/ppermute | solution.py:14
  239.8 9.2 %collective-permute-done.6 = bf16[2,512,128]{2,1,0:T(8,128)(2,1)S(1)} collective-permute-done((bf16[2,512,128]{2,1,0:T(8,128)(2,1)S(1)}, bf16[2,512,128]{2,1,0:T(8,128)(2,1)S(1)}, u32[]{:S(2)}, u32[]{:S(2)}) %collective-permute-start.6) | collective-permute-done | bytes 262176 | tf_op jit(solution)/shard_map/ppermute | solution.py:14
  249.7 67.9 %all-reduce.4.cloned.1.call-done = (f32[2,256,256]{2,1,0:T(8,128)}, f32[2,256,256]{2,1,0:T(8,128)}, f32[2,256,256]{2,1,0:T(8,128)}) async-done(((f32[2,256,256]{2,1,0:T(8,128)}, f32[2,256,256]{2,1,0:T(8,128)}, f32[2,256,256]{2,1,0:T(8,128)}), (f32[2,256,256]{2,1,0:T(8,128)}, f32[2,256,256]{2,1,0:T(8,128)}, f32[2,256,256]{2,1,0:T(8,128)})) %all-reduce.4.cloned.1.call-update) | async-done | bytes 1572880 | tf_op jit(solution)/shard_map/psum | solution.py:41
  317.6 1.1 multiply_bitcast_fusion.2
  318.7 1.3 multiply_bitcast_fusion
  320.0 1.2 pad_maximum_fusion
  (41 shorter events, 6.1 us)
Async XLA Ops:
  14.4 7.5 %copy-start.3 = (s32[3,2]{0,1:T(2,128)S(1)}, s32[3,2]{0,1:T(2,128)}, u32[]{:S(2)}) copy-start(s32[3,2]{0,1:T(2,128)} %param.5) | copy-start | bytes 76
  14.4 85.5 %all-to-all-start = ((bf16[3,128,4096]{1,0,2:T(4,128)(2,1)}), bf16[3,128,4096]{1,0,2:T(4,128)(2,1)}, u32[]{:S(2)}, u32[]{:S(2)}) async-start(bf16[3,128,4096]{1,0,2:T(4,128)(2,1)} %copy.39), calls=%async_computation | async-start | bytes 8388608 | tf_op jit(solution)/shard_map/all_to_all | solution.py:26
  21.9 295.7 %all-reduce.4.cloned.1.call-start = ((), (), s32[]{:S(2)}) async-start(), calls=%async_computation.1 | async-start | bytes 3145728 | tf_op jit(solution)/shard_map/psum | solution.py:41
  105.5 2.6 copy-start.4
  108.6 1.2 copy-start.1
  109.3 2.3 copy-start.2
  111.6 2.0 copy-start
  123.8 91.0 %collective-permute-start = (bf16[2,512,128]{2,1,0:T(8,128)(2,1)S(1)}, bf16[2,512,128]{2,1,0:T(8,128)(2,1)S(1)}, u32[]{:S(2)}, u32[]{:S(2)}) collective-permute-start(bf16[2,512,128]{2,1,0:T(8,128)(2,1)S(1)} %bitcast.154), channel_id=1, source_target_pairs={{15,0},{0,1},{1,2},{2,3},{3,4},{4,5},{5,6},{6,7},{7,8},{8,9},{9,10... | collective-permute-start | bytes 786440 | tf_op jit(solution)/shard_map/ppermute | solution.py:14
  129.5 86.1 %collective-permute-start.1 = (bf16[2,512,128]{2,1,0:T(8,128)(2,1)S(1)}, bf16[2,512,128]{2,1,0:T(8,128)(2,1)S(1)}, u32[]{:S(2)}, u32[]{:S(2)}) collective-permute-start(bf16[2,512,128]{2,1,0:T(8,128)(2,1)S(1)} %bitcast.153), channel_id=1, source_target_pairs={{14,0},{15,1},{0,2},{1,3},{2,4},{3,5},{4,6},{5,7},{6,8},{7,9},{8,1... | collective-permute-start | bytes 786440 | tf_op jit(solution)/shard_map/ppermute | solution.py:14
  139.6 79.0 %collective-permute-start.2 = (bf16[2,512,128]{2,1,0:T(8,128)(2,1)S(1)}, bf16[2,512,128]{2,1,0:T(8,128)(2,1)S(1)}, u32[]{:S(2)}, u32[]{:S(2)}) collective-permute-start(bf16[2,512,128]{2,1,0:T(8,128)(2,1)S(1)} %bitcast.152), channel_id=1, source_target_pairs={{13,0},{14,1},{15,2},{0,3},{1,4},{2,5},{3,6},{4,7},{5,8},{6,9},{7,... | collective-permute-start | bytes 786440 | tf_op jit(solution)/shard_map/ppermute | solution.py:14
  141.7 77.6 %collective-permute-start.3 = (bf16[2,512,128]{2,1,0:T(8,128)(2,1)S(1)}, bf16[2,512,128]{2,1,0:T(8,128)(2,1)S(1)}, u32[]{:S(2)}, u32[]{:S(2)}) collective-permute-start(bf16[2,512,128]{2,1,0:T(8,128)(2,1)S(1)} %bitcast.151), channel_id=1, source_target_pairs={{12,0},{13,1},{14,2},{15,3},{0,4},{1,5},{2,6},{3,7},{4,8},{5,9},{6... | collective-permute-start | bytes 786440 | tf_op jit(solution)/shard_map/ppermute | solution.py:14
  142.8 77.2 %collective-permute-start.4 = (bf16[2,512,128]{2,1,0:T(8,128)(2,1)S(1)}, bf16[2,512,128]{2,1,0:T(8,128)(2,1)S(1)}, u32[]{:S(2)}, u32[]{:S(2)}) collective-permute-start(bf16[2,512,128]{2,1,0:T(8,128)(2,1)S(1)} %bitcast.150), channel_id=1, source_target_pairs={{11,0},{12,1},{13,2},{14,3},{15,4},{0,5},{1,6},{2,7},{3,8},{4,9},{... | collective-permute-start | bytes 786440 | tf_op jit(solution)/shard_map/ppermute | solution.py:14
  214.8 24.2 %collective-permute-start.5 = (bf16[2,512,128]{2,1,0:T(8,128)(2,1)S(1)}, bf16[2,512,128]{2,1,0:T(8,128)(2,1)S(1)}, u32[]{:S(2)}, u32[]{:S(2)}) collective-permute-start(bf16[2,512,128]{2,1,0:T(8,128)(2,1)S(1)} %bitcast.156), channel_id=1, source_target_pairs={{10,0},{11,1},{12,2},{13,3},{14,4},{15,5},{0,6},{1,7},{2,8},{3,9},... | collective-permute-start | bytes 786440 | tf_op jit(solution)/shard_map/ppermute | solution.py:14
  215.6 33.3 %collective-permute-start.6 = (bf16[2,512,128]{2,1,0:T(8,128)(2,1)S(1)}, bf16[2,512,128]{2,1,0:T(8,128)(2,1)S(1)}, u32[]{:S(2)}, u32[]{:S(2)}) collective-permute-start(bf16[2,512,128]{2,1,0:T(8,128)(2,1)S(1)} %bitcast.155), channel_id=1, source_target_pairs={{9,0},{10,1},{11,2},{12,3},{13,4},{14,5},{15,6},{0,7},{1,8},{2,9},... | collective-permute-start | bytes 786440 | tf_op jit(solution)/shard_map/ppermute | solution.py:14
Sparse Core Ops, SparseCore 0:
  214.9 102.6 all-reduce.3
where the time goes:
time: 330 us; the launch traced here: 328 us
  waiting for transfers between devices  173 us (52%)
  blocking collectives  69.8 us (21%)
  starting transfers between devices  30 us (9%)
  local copies, waits for them, and re-layouts  24 us (7%)
  between operations  14.2 us (4%)
  matrix products  12.3 us (4%)
  other arithmetic  4.34 us (1%)
    all_to_all x1, waiting for transfers between devices, per_device(): lax.all_to_all(key_values, 'seq', split_axis=2, concat_axis=1, tiled=True)  77.9 us
    psum x1, blocking collectives, per_device(): gram_total, energy_total = lax.psum((gram_term, energy_term), 'seq')  69.8 us
    psum x1, waiting for transfers between devices, per_device(): gram_total, energy_total = lax.psum((gram_term, energy_term), 'seq')  67.9 us
    ppermute x7, waiting for transfers between devices, from_behind(): return lax.ppermute(block, axis, route)  27.5 us
    ppermute x7, starting transfers between devices, from_behind(): return lax.ppermute(block, axis, route)  22.5 us
    unnamed x27, local copies, waits for them, and re-layouts  15.8 us
    all_to_all x1, starting transfers between devices, per_device(): lax.all_to_all(key_values, 'seq', split_axis=2, concat_axis=1, tiled=True)  7.45 us
  transfers between devices with their start and end apart: 9, of which 4 were waited for; matrix products, arithmetic and copies ran while one was open for 2% of the time, Pallas kernels for 0%

commit v1 on v0

v1 whole, which is shorter than its diff:
```python
import functools

import jax
import jax.numpy as jnp
from jax import lax
from jax.experimental import pallas as pl
from jax.experimental.pallas import tpu as pltpu
from jax.sharding import PartitionSpec as P

REACH = 8
OWNER_SLOT_LIMIT = 2
CAP = 16
LANES = 128
MESH = pl.DeviceIdType.MESH


def loop(lo, hi, body):
    def step(i, carry):
        body(i)
        return carry

    lax.fori_loop(lo, hi, step, 0)


def kernel(
    n, layers, width, rank, span, piece, tokens,
    kv_ref, bases_ref, slot_ref,
    recv_ref, grams_ref, energies_ref,
    x_buf, basis_buf, coeff_buf, out_buf, slot_mine, slot_buf, part_buf, sum_buf, full_buf,
    basis_sem, own_sem, x_send, x_recv, slot_send, slot_recv, slot_own,
    rs_send, rs_recv, ag_send, ag_recv, mir_send, mir_recv, fwd_send, fwd_recv,
    out_send, out_recv, out_own,
):
    m = n // 2
    chunk = 2 * width // n
    me = lax.axis_index("seq")
    side = me // m
    q = lax.rem(me, m)
    base = side * m
    lrows = 2 * rank + width // LANES

    def remote(src, dst, send, recv, dev):
        return pltpu.make_async_remote_copy(
            src_ref=src, dst_ref=dst, send_sem=send, recv_sem=recv,
            device_id={"seq": dev}, device_id_type=MESH,
        )

    def basis_copy(l):
        return pltpu.make_async_copy(bases_ref.at[l, side], basis_buf.at[l], basis_sem.at[l])

    def own_copy(l):
        return pltpu.make_async_copy(
            kv_ref.at[l, :, pl.ds(pl.multiple_of(q * span, span), span)],
            x_buf.at[l, pl.ds(pl.multiple_of(q * chunk, chunk), chunk), :],
            own_sem.at[l],
        )

    def x_copy(l, r):
        to = lax.rem(q + r, m)
        return remote(
            kv_ref.at[l, :, pl.ds(pl.multiple_of(to * span, span), span)],
            x_buf.at[l, pl.ds(pl.multiple_of(q * chunk, chunk), chunk), :],
            x_send.at[l, r], x_recv.at[l, r], base + to,
        )

    barrier = pltpu.get_barrier_semaphore()

    def greet(r):
        pl.semaphore_signal(
            barrier, inc=1, device_id={"seq": lax.rem(me + r, n)}, device_id_type=MESH
        )

    for l in range(layers):
        basis_copy(l).start()
        own_copy(l).start()
    slot_mine[...] = jnp.zeros(slot_mine.shape, jnp.int32)
    for l in range(layers):
        for b in range(2):
            slot_mine[2 * l + b : 2 * l + b + 1, :] = jnp.full((1, LANES), slot_ref[l, b], jnp.int32)
    loop(1, n, greet)
    pl.semaphore_wait(barrier, n - 1)

    for l in range(layers):
        loop(1, m, lambda r: x_copy(l, r).start())

    lower = lax.rem(me, 2)

    def slot_copy(hh):
        return remote(
            slot_mine, slot_buf.at[lower], slot_send.at[hh], slot_recv.at[lower], hh * m + me // 2
        )

    def slot_local():
        return pltpu.make_async_copy(slot_mine, slot_buf.at[lower], slot_own)

    for hh in range(2):

        @pl.when(hh * m + me // 2 != me)
        def _():
            slot_copy(hh).start()

        @pl.when(hh * m + me // 2 == me)
        def _():
            slot_local().start()

    for l in range(layers):
        basis_copy(l).wait()
        own_copy(l).wait()
        loop(1, m, lambda r: x_copy(l, r).wait_recv())
        coeff = lax.dot_general(
            basis_buf[l], x_buf[l], (((0,), (0,)), ((), ())), preferred_element_type=jnp.float32
        ).astype(jnp.bfloat16)
        coeff_buf[l] = coeff
        gram = lax.dot_general(
            coeff, coeff, (((1,), (1,)), ((), ())), preferred_element_type=jnp.float32
        )
        top = l * lrows
        for j in range(rank // LANES):
            part_buf[top + j * rank : top + (j + 1) * rank, :] = gram[:, j * LANES : (j + 1) * LANES]
        top += 2 * rank
        rows = 256
        for c in range(width // rows):
            recon = jnp.dot(
                basis_buf[l, c * rows : (c + 1) * rows, :], coeff, preferred_element_type=jnp.float32
            )
            resid = x_buf[l, c * rows : (c + 1) * rows, :].astype(jnp.float32) - recon
            square = resid * resid
            folded = square[:, :LANES]
            for j in range(1, span // LANES):
                folded = folded + square[:, j * LANES : (j + 1) * LANES]
            line = jnp.sum(folded.T, axis=0, keepdims=True)
            for j in range(rows // LANES):
                at = top + c * (rows // LANES) + j
                part_buf[at : at + 1, :] = line[:, j * LANES : (j + 1) * LANES]

    total_rows = m * piece
    if total_rows > layers * lrows:
        part_buf[layers * lrows :, :] = jnp.zeros(
            (total_rows - layers * lrows, LANES), jnp.float32
        )

    def rows_of(i):
        return pl.ds(pl.multiple_of(i * piece, piece), piece)

    def rs_copy(r):
        to = lax.rem(q + r, m)
        return remote(
            part_buf.at[rows_of(to), :], sum_buf.at[r], rs_send.at[r], rs_recv.at[r], base + to
        )

    loop(1, m, lambda r: rs_copy(r).start())

    def slot_from(dd):
        return lax.rem(2 * q + dd, n)

    for dd in range(2):
        src_dev = 2 * q + dd

        @pl.when(src_dev != me)
        def _():
            remote(slot_mine, slot_buf.at[dd], slot_send.at[0], slot_recv.at[dd], me).wait_recv()

        @pl.when(src_dev == me)
        def _():
            pltpu.make_async_copy(slot_mine, slot_buf.at[dd], slot_own).wait()

    def out_dst(k):
        return recv_ref.at[
            pl.ds(OWNER_SLOT_LIMIT * k, OWNER_SLOT_LIMIT),
            pl.ds(pl.multiple_of(side * rank, rank), rank),
            :,
        ]

    def out_copy(dd, k):
        to = lax.rem(2 * q + dd + k, n)
        return remote(
            out_buf.at[dd, pl.ds(OWNER_SLOT_LIMIT * k, OWNER_SLOT_LIMIT)], out_dst(k),
            out_send.at[dd, k], out_recv.at[side, k], to,
        )

    def out_local(dd, k):
        return pltpu.make_async_copy(
            out_buf.at[dd, pl.ds(OWNER_SLOT_LIMIT * k, OWNER_SLOT_LIMIT)], out_dst(k), out_own.at[dd]
        )

    for k in reversed(range(REACH)):
        for dd in range(2):
            for w in range(OWNER_SLOT_LIMIT):
                v = OWNER_SLOT_LIMIT * k + w
                acc = None
                for l in range(layers):
                    for b in range(2):
                        pick = slot_buf[dd, 2 * l + b : 2 * l + b + 1, :] == v
                        pick = pick.astype(jnp.float32).astype(jnp.bfloat16)
                        at = (2 * dd + b) * LANES
                        term = coeff_buf[l, :, at : at + LANES] * pick
                        acc = term if acc is None else acc + term
                out_buf[dd, v] = acc
            to = lax.rem(2 * q + dd + k, n)

            @pl.when(to != me)
            def _():
                out_copy(dd, k).start()

            @pl.when(to == me)
            def _():
                out_local(dd, k).start()

    loop(1, m, lambda r: rs_copy(r).wait())
    total = part_buf[rows_of(q), :]
    for r in range(1, m):
        total = total + sum_buf[r]
    full_buf[side, rows_of(q), :] = total

    def ag_copy(r):
        at = full_buf.at[side, rows_of(q), :]
        return remote(at, at, ag_send.at[r], ag_recv.at[r], base + lax.rem(q + r, m))

    def mirror_copy():
        at = full_buf.at[side, rows_of(q), :]
        return remote(at, at, mir_send, mir_recv, (1 - side) * m + q)

    def fwd_copy(r):
        at = full_buf.at[1 - side, rows_of(q), :]
        return remote(at, at, fwd_send.at[r], fwd_recv.at[r], base + lax.rem(q + r, m))

    mirror_copy().start()
    loop(1, m, lambda r: ag_copy(r).start())
    mirror_copy().wait()
    loop(1, m, lambda r: fwd_copy(r).start())
    loop(1, m, lambda r: ag_copy(r).wait())
    loop(1, m, lambda r: fwd_copy(r).wait())

    scale = 1.0 / tokens
    for s in range(2):
        for l in range(layers):
            top = l * lrows
            for j in range(rank // LANES):
                grams_ref[l, s, :, j * LANES : (j + 1) * LANES] = (
                    full_buf[s, top + j * rank : top + (j + 1) * rank, :] * scale
                )
            top += 2 * rank
            for j in range(width // LANES):
                energies_ref[l, s : s + 1, j * LANES : (j + 1) * LANES] = (
                    full_buf[s, top + j : top + j + 1, :] * scale
                )

    for hh in range(2):

        @pl.when(hh * m + me // 2 != me)
        def _():
            slot_copy(hh).wait_send()

    for l in range(layers):
        loop(1, m, lambda r: x_copy(l, r).wait_send())
    for dd in range(2):
        for k in range(REACH):
            to = lax.rem(2 * q + dd + k, n)

            @pl.when(to != me)
            def _():
                out_copy(dd, k).wait_send()

            @pl.when(to == me)
            def _():
                out_local(dd, k).wait()

    for hh in range(2):
        for k in range(REACH):
            sender = hh * m + lax.rem(me - k + n, n) // 2

            @pl.when(sender != me)
            def _():
                at = recv_ref.at[
                    pl.ds(OWNER_SLOT_LIMIT * k, OWNER_SLOT_LIMIT), pl.ds(hh * rank, rank), :
                ]
                remote(at, at, out_send.at[0, 0], out_recv.at[hh, k], me).wait_recv()


def per_device(key_values, bases, owner_slots):
    n = lax.axis_size("seq")
    layers, chunk, tokens = key_values.shape
    width, rank = bases.shape[2], bases.shape[3]
    m = n // 2
    span = tokens // m
    lrows = 2 * rank + width // LANES
    piece = -(-layers * lrows // (8 * m)) * 8
    unit = LANES
    vmem = pltpu.VMEM
    dma = pltpu.SemaphoreType.DMA
    any_space = pl.BlockSpec(memory_space=pl.ANY)
    in_vmem = pl.BlockSpec(memory_space=pltpu.VMEM)
    return pl.pallas_call(
        functools.partial(kernel, n, layers, width, rank, span, piece, tokens),
        out_shape=(
            jax.ShapeDtypeStruct((CAP, 2 * rank, unit), jnp.bfloat16),
            jax.ShapeDtypeStruct((layers, 2, rank, rank), jnp.float32),
            jax.ShapeDtypeStruct((layers, 2, width), jnp.float32),
        ),
        in_specs=[any_space, any_space, pl.BlockSpec(memory_space=pltpu.SMEM)],
        out_specs=(any_space, in_vmem, in_vmem),
        scratch_shapes=[
            vmem((layers, width, span), jnp.bfloat16),
            vmem((layers, width, rank), jnp.bfloat16),
            vmem((layers, rank, span), jnp.bfloat16),
            vmem((2, CAP, rank, unit), jnp.bfloat16),
            vmem((8, LANES), jnp.int32),
            vmem((2, 8, LANES), jnp.int32),
            vmem((m * piece, LANES), jnp.float32),
            vmem((m, piece, LANES), jnp.float32),
            vmem((2, m * piece, LANES), jnp.float32),
            dma((layers,)), dma((layers,)), dma((layers, m)), dma((layers, m)),
            dma((2,)), dma((2,)), dma,
            dma((m,)), dma((m,)), dma((m,)), dma((m,)), dma, dma, dma((m,)), dma((m,)),
            dma((2, REACH)), dma((2, REACH)), dma((2,)),
        ],
        compiler_params=pltpu.CompilerParams(
            collective_id=0, has_side_effects=True, vmem_limit_bytes=40 * 1024 * 1024
        ),
        name="compress_handoff",
    )(key_values, bases, owner_slots)


def solution(mesh):
    in_specs = (P(None, "seq", "groups"), P(), P(None, ("groups", "seq")))
    out_specs = (
        P(("groups", "seq"), None, None),
        P("groups", None, None, None),
        P("groups", None, None),
    )
    return jax.shard_map(
        per_device, mesh=mesh, in_specs=in_specs, out_specs=out_specs, check_vma=False
    )
```

time: 330 us -> 126 us (0.38)
  waiting for transfers between devices: 173 us -> 0 us
  Pallas kernels: 0 us -> 117 us
  blocking collectives: 69.8 us -> 0 us
  starting transfers between devices: 30 us -> 0 us
  local copies, waits for them, and re-layouts: 24 us -> 7.61 us
  between operations: 14.2 us -> 0.64 us
  matrix products: 12.3 us -> 0 us
  other arithmetic: 4.34 us -> 0 us
    pallas_call x0 -> x1, Pallas kernels: none -> 117 us  [per_device(): pl.pallas_call(functools.partial(kernel, n, layers, width, rank, span, pi...]
    all_to_all x1 -> x0, waiting for transfers between devices: 77.9 us -> none  [per_device(): lax.all_to_all(key_values, 'seq', split_axis=2, concat_axis=1, tiled=True)]
    psum x1 -> x0, blocking collectives: 69.8 us -> none  [per_device(): gram_total, energy_total = lax.psum((gram_term, energy_term), 'seq')]
    psum x1 -> x0, waiting for transfers between devices: 67.9 us -> none  [per_device(): gram_total, energy_total = lax.psum((gram_term, energy_term), 'seq')]
    ppermute x7 -> x0, waiting for transfers between devices: 27.5 us -> none  [from_behind(): return lax.ppermute(block, axis, route)]
    ppermute x7 -> x0, starting transfers between devices: 22.5 us -> none  [from_behind(): return lax.ppermute(block, axis, route)]
    dot_general x10 -> x0, matrix products: 12.3 us -> none  [the longest x3 4.23 us: per_device(): jnp.einsum('scr,srt->sct', basis, coeff, preferred_element_type=jnp.float32)]
    unnamed x27 -> x8, local copies, waits for them, and re-layouts: 15.8 us -> 7.61 us
  transfers between devices with their start and end apart: 9 -> 0, of which waited for: 4 -> 0; matrix products, arithmetic and copies ran while one was open for 2% -> 0% of each run, Pallas kernels for 0% -> 0%
where the time goes in v1:
time: 126 us; the launch traced here: 125 us
  Pallas kernels  117 us (93%)
  local copies, waits for them, and re-layouts  7.61 us (6%)
    pallas_call x1, Pallas kernels, per_device(): pl.pallas_call(functools.partial(kernel, n, layers, width, rank, span, pi...  117 us
    unnamed x8, local copies, waits for them, and re-layouts  7.61 us

profile of v1, /device:TPU:1, one launch (start us, length us, event | category | flops | bytes accessed | tf_op | source)
XLA Modules:
  0.0 124.8 jit_solution(9586462882639174862)
XLA Ops:
  0.6 0.8 copy.6.slot_ref
  1.4 0.0 copy-start
  1.4 1.9 %copy-done = bf16[3,128,4096]{2,1,0:T(8,128)(2,1)S(1)} copy-done((bf16[3,128,4096]{2,1,0:T(8,128)(2,1)S(1)}, bf16[3,128,4096]{2,1,0:T(8,128)(2,1)}, u32[]{:S(2)}) %copy-start) | copy-done | bytes 3145752
  3.3 0.0 copy-start.1
  3.3 1.9 %copy-done.1 = bf16[3,2,1024,256]{3,2,1,0:T(8,128)(2,1)S(1)} copy-done((bf16[3,2,1024,256]{3,2,1,0:T(8,128)(2,1)S(1)}, bf16[3,2,1024,256]{3,2,1,0:T(8,128)(2,1)}, u32[]{:S(2)}) %copy-start.1) | copy-done | bytes 3145752
  5.2 116.5 %compress_handoff.1 = (bf16[16,512,128]{2,1,0:T(8,128)(2,1)S(1)}, f32[3,2,256,256]{3,2,1,0:T(8,128)S(1)}, f32[3,2,1024]{2,1,0:T(2,128)S(1)}) custom-call(bf16[3,128,4096]{2,1,0:T(8,128)(2,1)S(1)} %copy-done, bf16[3,2,1024,256]{3,2,1,0:T(8,128)(2,1)S(1)} %copy-done.1, s32[3,2]{1,0:T(4,128)S(1)} %copy.6.slot_ref), custom_call_target="tpu_custom_call" | custom-call | tf_op jit(solution)/shard_map/compress_handoff/pallas_call | solution.py:293
  121.7 1.3 %copy.10 = bf16[16,512,128]{2,1,0:T(8,128)(2,1)} copy(bf16[16,512,128]{2,1,0:T(8,128)(2,1)S(1)} %get-tuple-element.6) | data formatting | bytes 4194304
  123.0 1.1 copy.11
  124.2 0.6 copy.12
Async XLA Ops:
  1.4 1.9 %copy-start = (bf16[3,128,4096]{2,1,0:T(8,128)(2,1)S(1)}, bf16[3,128,4096]{2,1,0:T(8,128)(2,1)}, u32[]{:S(2)}) copy-start(bf16[3,128,4096]{2,1,0:T(8,128)(2,1)} %kv_ref.1) | copy-start | bytes 9437188
  3.3 1.9 %copy-start.1 = (bf16[3,2,1024,256]{3,2,1,0:T(8,128)(2,1)S(1)}, bf16[3,2,1024,256]{3,2,1,0:T(8,128)(2,1)}, u32[]{:S(2)}) copy-start(bf16[3,2,1024,256]{3,2,1,0:T(8,128)(2,1)} %bases_ref.1) | copy-start | bytes 9437188

commit v2 on v1

v2 whole, which is shorter than its diff:
```python
import functools

import jax
import jax.numpy as jnp
from jax import lax
from jax.experimental import pallas as pl
from jax.experimental.pallas import tpu as pltpu
from jax.sharding import PartitionSpec as P

REACH = 8
OWNER_SLOT_LIMIT = 2
CAP = 16
LANES = 128
MESH = pl.DeviceIdType.MESH


def loop(lo, hi, body):
    def step(i, carry):
        body(i)
        return carry

    lax.fori_loop(lo, hi, step, 0)


def kernel(
    n, layers, width, rank, span, piece, tokens,
    kv_ref, bases_ref, slot_ref,
    recv_ref, grams_ref, energies_ref,
    x_buf, basis_buf, coeff_buf, out_buf, slot_mine, slot_buf, part_buf, pair_buf, sum_buf, full_buf,
    basis_sem, own_sem, x_send, x_recv, slot_send, slot_recv, slot_own,
    pair_send, pair_recv, rs_send, rs_recv, ag_send, ag_recv, mir_send, mir_recv, fwd_send, fwd_recv,
    sib_send, sib_recv, out_send, out_recv, out_own,
):
    m = n // 2
    chips = m // 2
    turn = n // 4
    chunk = 2 * width // n
    me = lax.axis_index("seq")
    side = me // m
    q = lax.rem(me, m)
    base = side * m
    chip = q // 2
    core = lax.rem(q, 2)
    sibling = me + 1 - 2 * core
    lrows = 2 * rank + width // LANES

    def remote(src, dst, send, recv, dev):
        return pltpu.make_async_remote_copy(
            src_ref=src, dst_ref=dst, send_sem=send, recv_sem=recv,
            device_id={"seq": dev}, device_id_type=MESH,
        )

    def held(i, dd):
        return lax.rem(2 * i + dd + n - turn, n)

    def holder(d):
        return lax.rem(d + turn, n) // 2

    def basis_copy(l):
        return pltpu.make_async_copy(bases_ref.at[l, side], basis_buf.at[l], basis_sem.at[l])

    def kv_at(l, i, dd):
        return kv_ref.at[l, :, pl.ds(pl.multiple_of(held(i, dd) * span, span), span)]

    def x_at(l, dd):
        return x_buf.at[dd, l, pl.ds(pl.multiple_of(q * chunk, chunk), chunk), :]

    def own_copy(l, dd):
        return pltpu.make_async_copy(kv_at(l, q, dd), x_at(l, dd), own_sem.at[dd, l])

    def x_copy(l, dd, r):
        to = lax.rem(q + r, m)
        return remote(
            kv_at(l, to, dd), x_at(l, dd), x_send.at[dd, l, r], x_recv.at[dd, l, r], base + to
        )

    barrier = pltpu.get_barrier_semaphore()

    def greet(r):
        pl.semaphore_signal(
            barrier, inc=1, device_id={"seq": lax.rem(me + r, n)}, device_id_type=MESH
        )

    loop(1, n, greet)
    for l in range(layers):
        basis_copy(l).start()
        for dd in range(2):
            own_copy(l, dd).start()
    slot_mine[...] = jnp.zeros(slot_mine.shape, jnp.int32)
    for l in range(layers):
        for b in range(2):
            slot_mine[2 * l + b : 2 * l + b + 1, :] = jnp.full((1, LANES), slot_ref[l, b], jnp.int32)
    pl.semaphore_wait(barrier, n - 1)

    for dd in range(2):
        for l in range(layers):
            loop(1, m, lambda r: x_copy(l, dd, r).start())

    lower = lax.rem(me + turn, 2)

    def slot_copy(hh):
        return remote(
            slot_mine, slot_buf.at[lower], slot_send.at[hh], slot_recv.at[lower],
            hh * m + holder(me),
        )

    def slot_local():
        return pltpu.make_async_copy(slot_mine, slot_buf.at[lower], slot_own)

    for hh in range(2):

        @pl.when(hh * m + holder(me) != me)
        def _():
            slot_copy(hh).start()

        @pl.when(hh * m + holder(me) == me)
        def _():
            slot_local().start()

    def out_dst(k):
        return recv_ref.at[
            pl.ds(OWNER_SLOT_LIMIT * k, OWNER_SLOT_LIMIT),
            pl.ds(pl.multiple_of(side * rank, rank), rank),
            :,
        ]

    def out_copy(dd, k):
        return remote(
            out_buf.at[dd, pl.ds(OWNER_SLOT_LIMIT * k, OWNER_SLOT_LIMIT)], out_dst(k),
            out_send.at[dd, k], out_recv.at[side, k], lax.rem(held(q, dd) + k, n),
        )

    def out_local(dd, k):
        return pltpu.make_async_copy(
            out_buf.at[dd, pl.ds(OWNER_SLOT_LIMIT * k, OWNER_SLOT_LIMIT)], out_dst(k), out_own.at[dd]
        )

    half_rows = chips * piece
    total_rows = m * piece
    if total_rows > layers * lrows:
        part_buf[layers * lrows :, :] = jnp.zeros(
            (total_rows - layers * lrows, LANES), jnp.float32
        )

    def half_of(b):
        return pl.ds(pl.multiple_of(b * half_rows, piece), half_rows)

    def rows_of(c):
        return pl.ds(pl.multiple_of(core * half_rows + c * piece, piece), piece)

    def pair_copy():
        return remote(part_buf.at[half_of(1 - core), :], pair_buf, pair_send, pair_recv, sibling)

    def emit(dd, ks):
        src_dev = held(q, dd)
        for k in ks:
            for w in range(OWNER_SLOT_LIMIT):
                v = OWNER_SLOT_LIMIT * k + w
                acc = None
                for l in range(layers):
                    for b in range(2):
                        pick = slot_buf[dd, 2 * l + b : 2 * l + b + 1, :] == v
                        pick = pick.astype(jnp.float32).astype(jnp.bfloat16)
                        term = coeff_buf[l, :, b * LANES : (b + 1) * LANES] * pick
                        acc = term if acc is None else acc + term
                out_buf[dd, v] = acc
            to = lax.rem(src_dev + k, n)

            @pl.when(to != me)
            def _():
                out_copy(dd, k).start()

            @pl.when(to == me)
            def _():
                out_local(dd, k).start()

    def rs_copy(r):
        to = lax.rem(chip + r, chips)
        return remote(
            part_buf.at[rows_of(to), :], sum_buf.at[r], rs_send.at[r], rs_recv.at[r],
            base + 2 * to + core,
        )

    def ag_copy(r):
        at = full_buf.at[side, rows_of(chip), :]
        return remote(
            at, at, ag_send.at[r], ag_recv.at[r], base + 2 * lax.rem(chip + r, chips) + core
        )

    def mirror_copy():
        at = full_buf.at[side, rows_of(chip), :]
        return remote(at, at, mir_send, mir_recv, (1 - side) * m + q)

    def fwd_copy(r):
        at = full_buf.at[1 - side, rows_of(chip), :]
        return remote(
            at, at, fwd_send.at[r], fwd_recv.at[r], base + 2 * lax.rem(chip + r, chips) + core
        )

    def sib_copy(s):
        at = full_buf.at[s, half_of(core), :]
        return remote(at, at, sib_send.at[s], sib_recv.at[s], sibling)

    for dd in range(2):
        for l in range(layers):
            if dd == 0:
                basis_copy(l).wait()
            own_copy(l, dd).wait()
            loop(1, m, lambda r: x_copy(l, dd, r).wait_recv())
            coeff = lax.dot_general(
                basis_buf[l], x_buf[dd, l], (((0,), (0,)), ((), ())),
                preferred_element_type=jnp.float32,
            ).astype(jnp.bfloat16)
            coeff_buf[l] = coeff
            gram = lax.dot_general(
                coeff, coeff, (((1,), (1,)), ((), ())), preferred_element_type=jnp.float32
            )

            def put(at, value):
                if dd == 0:
                    part_buf[at : at + value.shape[0], :] = value
                else:
                    part_buf[at : at + value.shape[0], :] += value

            top = l * lrows
            for j in range(rank // LANES):
                put(top + j * rank, gram[:, j * LANES : (j + 1) * LANES])
            top += 2 * rank
            rows = 256
            for c in range(width // rows):
                recon = jnp.dot(
                    basis_buf[l, c * rows : (c + 1) * rows, :], coeff,
                    preferred_element_type=jnp.float32,
                )
                resid = x_buf[dd, l, c * rows : (c + 1) * rows, :].astype(jnp.float32) - recon
                square = resid * resid
                folded = square[:, :LANES]
                for j in range(1, span // LANES):
                    folded = folded + square[:, j * LANES : (j + 1) * LANES]
                line = jnp.sum(folded.T, axis=0, keepdims=True)
                for j in range(rows // LANES):
                    put(top + c * (rows // LANES) + j, line[:, j * LANES : (j + 1) * LANES])

        if dd == 1:
            pair_copy().start()

        src_dev = held(q, dd)

        @pl.when(src_dev != me)
        def _():
            remote(slot_mine, slot_buf.at[dd], slot_send.at[0], slot_recv.at[dd], me).wait_recv()

        @pl.when(src_dev == me)
        def _():
            pltpu.make_async_copy(slot_mine, slot_buf.at[dd], slot_own).wait()

        if dd == 0:
            emit(0, range(REACH - 1, -1, -1))

    ks = list(range(REACH - 1, -1, -1))
    emit(1, ks[:2])
    pair_copy().wait()
    part_buf[half_of(core), :] += pair_buf[...]
    loop(1, chips, lambda r: rs_copy(r).start())
    emit(1, ks[2:4])
    loop(1, chips, lambda r: rs_copy(r).wait())
    total = part_buf[rows_of(chip), :]
    for r in range(1, chips):
        total = total + sum_buf[r]
    full_buf[side, rows_of(chip), :] = total
    mirror_copy().start()
    loop(1, chips, lambda r: ag_copy(r).start())
    emit(1, ks[4:6])
    loop(1, chips, lambda r: ag_copy(r).wait_recv())
    sib_copy(side).start()
    mirror_copy().wait_recv()
    loop(1, chips, lambda r: fwd_copy(r).start())
    emit(1, ks[6:])
    loop(1, chips, lambda r: fwd_copy(r).wait_recv())
    sib_copy(1 - side).start()
    sib_copy(0).wait()
    sib_copy(1).wait()

    scale = 1.0 / tokens
    for s in range(2):
        for l in range(layers):
            top = l * lrows
            for j in range(rank // LANES):
                grams_ref[l, s, :, j * LANES : (j + 1) * LANES] = (
                    full_buf[s, top + j * rank : top + (j + 1) * rank, :] * scale
                )
            top += 2 * rank
            for j in range(width // LANES):
                energies_ref[l, s : s + 1, j * LANES : (j + 1) * LANES] = (
                    full_buf[s, top + j : top + j + 1, :] * scale
                )

    mirror_copy().wait_send()
    loop(1, chips, lambda r: ag_copy(r).wait_send())
    loop(1, chips, lambda r: fwd_copy(r).wait_send())
    for hh in range(2):

        @pl.when(hh * m + holder(me) != me)
        def _():
            slot_copy(hh).wait_send()

    for dd in range(2):
        for l in range(layers):
            loop(1, m, lambda r: x_copy(l, dd, r).wait_send())
        for k in range(REACH):
            to = lax.rem(held(q, dd) + k, n)

            @pl.when(to != me)
            def _():
                out_copy(dd, k).wait_send()

            @pl.when(to == me)
            def _():
                out_local(dd, k).wait()

    for hh in range(2):
        for k in range(REACH):
            sender = hh * m + holder(lax.rem(me - k + n, n))

            @pl.when(sender != me)
            def _():
                at = recv_ref.at[
                    pl.ds(OWNER_SLOT_LIMIT * k, OWNER_SLOT_LIMIT), pl.ds(hh * rank, rank), :
                ]
                remote(at, at, out_send.at[0, 0], out_recv.at[hh, k], me).wait_recv()


def per_device(key_values, bases, owner_slots):
    n = lax.axis_size("seq")
    layers, chunk, tokens = key_values.shape
    width, rank = bases.shape[2], bases.shape[3]
    m = n // 2
    chips = m // 2
    span = tokens // n
    lrows = 2 * rank + width // LANES
    piece = -(-layers * lrows // (8 * m)) * 8
    unit = LANES
    vmem = pltpu.VMEM
    dma = pltpu.SemaphoreType.DMA
    any_space = pl.BlockSpec(memory_space=pl.ANY)
    in_vmem = pl.BlockSpec(memory_space=pltpu.VMEM)
    return pl.pallas_call(
        functools.partial(kernel, n, layers, width, rank, span, piece, tokens),
        out_shape=(
            jax.ShapeDtypeStruct((CAP, 2 * rank, unit), jnp.bfloat16),
            jax.ShapeDtypeStruct((layers, 2, rank, rank), jnp.float32),
            jax.ShapeDtypeStruct((layers, 2, width), jnp.float32),
        ),
        in_specs=[any_space, any_space, pl.BlockSpec(memory_space=pltpu.SMEM)],
        out_specs=(any_space, in_vmem, in_vmem),
        scratch_shapes=[
            vmem((2, layers, width, span), jnp.bfloat16),
            vmem((layers, width, rank), jnp.bfloat16),
            vmem((layers, rank, span), jnp.bfloat16),
            vmem((2, CAP, rank, unit), jnp.bfloat16),
            vmem((8, LANES), jnp.int32),
            vmem((2, 8, LANES), jnp.int32),
            vmem((m * piece, LANES), jnp.float32),
            vmem((chips * piece, LANES), jnp.float32),
            vmem((chips, piece, LANES), jnp.float32),
            vmem((2, m * piece, LANES), jnp.float32),
            dma((layers,)), dma((2, layers)), dma((2, layers, m)), dma((2, layers, m)),
            dma((2,)), dma((2,)), dma,
            dma, dma, dma((chips,)), dma((chips,)), dma((chips,)), dma((chips,)), dma, dma,
            dma((chips,)), dma((chips,)),
            dma((2,)), dma((2,)), dma((2, REACH)), dma((2, REACH)), dma((2,)),
        ],
        compiler_params=pltpu.CompilerParams(
            collective_id=0, has_side_effects=True, vmem_limit_bytes=58 * 1024 * 1024
        ),
        name="compress_handoff",
    )(key_values, bases, owner_slots)


def solution(mesh):
    in_specs = (P(None, "seq", "groups"), P(), P(None, ("groups", "seq")))
    out_specs = (
        P(("groups", "seq"), None, None),
        P("groups", None, None, None),
        P("groups", None, None),
    )
    return jax.shard_map(
        per_device, mesh=mesh, in_specs=in_specs, out_specs=out_specs, check_vma=False
    )
```

time: 126 us -> 108 us (0.86); the launches traced: 125 us -> 108 us
  Pallas kernels: 117 us -> 101 us
  local copies, waits for them, and re-layouts: 7.61 us -> 6.32 us
    pallas_call x1, Pallas kernels: 117 us -> 101 us  [per_device(): pl.pallas_call(functools.partial(kernel, n, layers, width, rank, span, pi...]
    unnamed x8, local copies, waits for them, and re-layouts: 7.61 us -> 6.32 us
where the time goes in v2:
time: 108 us
  Pallas kernels  101 us (94%)
  local copies, waits for them, and re-layouts  6.32 us (6%)
    pallas_call x1, Pallas kernels, per_device(): pl.pallas_call(functools.partial(kernel, n, layers, width, rank, span, pi...  101 us
    unnamed x8, local copies, waits for them, and re-layouts  6.32 us

profile of v2, /device:TPU:1, one launch (start us, length us, event | category | flops | bytes accessed | tf_op | source)
XLA Modules:
  0.0 108.0 jit_solution(12945857402366871837)
XLA Ops:
  0.6 1.3 %copy.6.slot_ref = s32[3,2]{1,0:T(4,128)} copy(s32[3,2]{0,1:T(2,128)} %param.5) | data formatting | bytes 48 | tf_op args[2]
  2.0 101.1 %compress_handoff.1 = (bf16[16,512,128]{2,1,0:T(8,128)(2,1)}, f32[3,2,256,256]{3,2,1,0:T(8,128)}, f32[3,2,1024]{2,1,0:T(2,128)}) custom-call(bf16[3,128,4096]{2,1,0:T(8,128)(2,1)} %kv_ref.1, bf16[3,2,1024,256]{3,2,1,0:T(8,128)(2,1)} %bases_ref.1, s32[3,2]{1,0:T(4,128)} %copy.6.slot_ref), custom_call_target="tpu_custom_call" | custom-call | tf_op jit(solution)/shard_map/compress_handoff/pallas_call | solution.py:347
  103.0 0.0 copy-start
  103.1 3.2 %copy.10 = bf16[16,512,128]{2,1,0:T(8,128)(2,1)} copy(bf16[16,512,128]{2,1,0:T(8,128)(2,1)} %get-tuple-element.6) | data formatting | bytes 4194304
  106.3 0.0 copy-done
  106.3 0.0 copy-start.1
  106.3 1.1 %copy.11 = f32[3,2,256,256]{3,2,1,0:T(8,128)} copy(f32[3,2,256,256]{3,2,1,0:T(8,128)S(1)} %copy-done) | data formatting | bytes 3145728
  107.4 0.0 copy-done.1
  107.4 0.6 copy.12
Async XLA Ops:
  103.0 3.2 %copy-start = (f32[3,2,256,256]{3,2,1,0:T(8,128)S(1)}, f32[3,2,256,256]{3,2,1,0:T(8,128)}, u32[]{:S(2)}) copy-start(f32[3,2,256,256]{3,2,1,0:T(8,128)} %get-tuple-element.7) | copy-start | bytes 4718596
  106.3 1.1 %copy-start.1 = (f32[3,2,1024]{2,1,0:T(2,128)S(1)}, f32[3,2,1024]{2,1,0:T(2,128)}, u32[]{:S(2)}) copy-start(f32[3,2,1024]{2,1,0:T(2,128)} %get-tuple-element.8) | copy-start | bytes 73732

commit v3 on v2

--- a/solution.py
+++ b/solution.py
@@ -26,10 +26,10 @@
     n, layers, width, rank, span, piece, tokens,
     kv_ref, bases_ref, slot_ref,
     recv_ref, grams_ref, energies_ref,
-    x_buf, basis_buf, coeff_buf, out_buf, slot_mine, slot_buf, part_buf, pair_buf, sum_buf, full_buf,
+    x_buf, basis_buf, coeff_buf, raw_buf, out_buf, slot_mine, slot_buf, raw_slot, part_buf, pair_buf, sum_buf, full_buf,
     basis_sem, own_sem, x_send, x_recv, slot_send, slot_recv, slot_own,
     pair_send, pair_recv, rs_send, rs_recv, ag_send, ag_recv, mir_send, mir_recv, fwd_send, fwd_recv,
-    sib_send, sib_recv, out_send, out_recv, out_own,
+    sib_send, sib_recv, raw_send, raw_recv, raw_slot_send, raw_slot_recv, out_send, out_recv, out_own,
 ):
     m = n // 2
     chips = m // 2
@@ -43,6 +43,10 @@
     core = lax.rem(q, 2)
     sibling = me + 1 - 2 * core
     lrows = 2 * rank + width // LANES
+    step = (1 - 2 * side) * (m // 2)
+    partner = me + step
+    partner_q = q - step
+    inner = q // (m // 2) == 1 - side
 
     def remote(src, dst, send, recv, dev):
         return pltpu.make_async_remote_copy(
@@ -117,23 +121,40 @@
         def _():
             slot_local().start()
 
-    def out_dst(k):
-        return recv_ref.at[
-            pl.ds(OWNER_SLOT_LIMIT * k, OWNER_SLOT_LIMIT),
-            pl.ds(pl.multiple_of(side * rank, rank), rank),
-            :,
-        ]
-
-    def out_copy(dd, k):
-        return remote(
-            out_buf.at[dd, pl.ds(OWNER_SLOT_LIMIT * k, OWNER_SLOT_LIMIT)], out_dst(k),
-            out_send.at[dd, k], out_recv.at[side, k], lax.rem(held(q, dd) + k, n),
-        )
-
-    def out_local(dd, k):
-        return pltpu.make_async_copy(
-            out_buf.at[dd, pl.ds(OWNER_SLOT_LIMIT * k, OWNER_SLOT_LIMIT)], out_dst(k), out_own.at[dd]
-        )
+    def raw_copy(dd, l):
+        return remote(
+            coeff_buf.at[dd, l], raw_buf.at[dd, l], raw_send.at[dd, l], raw_recv.at[dd, l], partner
+        )
+
+    def raw_slot_copy(dd):
+        return remote(
+            slot_buf.at[dd], raw_slot.at[dd], raw_slot_send.at[dd], raw_slot_recv.at[dd], partner
+        )
+
+    def owner(relay, dd, k):
+        return lax.rem(held(partner_q if relay else q, dd) + k, n)
+
+    def is_sent(relay, dd, k):
+        near = owner(relay, dd, k) // m == side
+        if relay:
+            return jnp.logical_and(inner, near)
+        return jnp.logical_or(jnp.logical_not(inner), near)
+
+    def out_refs(relay, dd, k):
+        part = 1 - side if relay else side
+        slots = pl.ds(OWNER_SLOT_LIMIT * k, OWNER_SLOT_LIMIT)
+        dst = recv_ref.at[slots, pl.ds(pl.multiple_of(part * rank, rank), rank), :]
+        return part, out_buf.at[int(relay), dd, slots], dst
+
+    def out_copy(relay, dd, k):
+        part, src, dst = out_refs(relay, dd, k)
+        return remote(
+            src, dst, out_send.at[int(relay), dd, k], out_recv.at[part, k], owner(relay, dd, k)
+        )
+
+    def out_local(relay, dd, k):
+        part, src, dst = out_refs(relay, dd, k)
+        return pltpu.make_async_copy(src, dst, out_own.at[int(relay), dd])
 
     half_rows = chips * piece
     total_rows = m * piece
@@ -151,28 +172,38 @@
     def pair_copy():
         return remote(part_buf.at[half_of(1 - core), :], pair_buf, pair_send, pair_recv, sibling)
 
-    def emit(dd, ks):
-        src_dev = held(q, dd)
+    def emit(relay, dd, ks):
+        units = raw_buf if relay else coeff_buf
+        numbers = raw_slot if relay else slot_buf
         for k in ks:
-            for w in range(OWNER_SLOT_LIMIT):
-                v = OWNER_SLOT_LIMIT * k + w
-                acc = None
-                for l in range(layers):
-                    for b in range(2):
-                        pick = slot_buf[dd, 2 * l + b : 2 * l + b + 1, :] == v
-                        pick = pick.astype(jnp.float32).astype(jnp.bfloat16)
-                        term = coeff_buf[l, :, b * LANES : (b + 1) * LANES] * pick
-                        acc = term if acc is None else acc + term
-                out_buf[dd, v] = acc
-            to = lax.rem(src_dev + k, n)
-
-            @pl.when(to != me)
+
+            @pl.when(is_sent(relay, dd, k))
             def _():
-                out_copy(dd, k).start()
-
-            @pl.when(to == me)
-            def _():
-                out_local(dd, k).start()
+                for w in range(OWNER_SLOT_LIMIT):
+                    v = OWNER_SLOT_LIMIT * k + w
+                    acc = None
+                    for l in range(layers):
+                        for b in range(2):
+                            pick = numbers[dd, 2 * l + b : 2 * l + b + 1, :] == v
+                            pick = pick.astype(jnp.float32).astype(jnp.bfloat16)
+                            term = units[dd, l, :, b * LANES : (b + 1) * LANES] * pick
+                            acc = term if acc is None else acc + term
+                    out_buf[int(relay), dd, v] = acc
+
+                @pl.when(owner(relay, dd, k) != me)
+                def _():
+                    out_copy(relay, dd, k).start()
+
+                @pl.when(owner(relay, dd, k) == me)
+                def _():
+                    out_local(relay, dd, k).start()
+
+    def take_raw(dd):
+        @pl.when(inner)
+        def _():
+            for l in range(layers):
+                raw_copy(dd, l).wait_recv()
+            raw_slot_copy(dd).wait_recv()
 
     def rs_copy(r):
         to = lax.rem(chip + r, chips)
@@ -201,8 +232,12 @@
         at = full_buf.at[s, half_of(core), :]
         return remote(at, at, sib_send.at[s], sib_recv.at[s], sibling)
 
+    ks = list(range(REACH - 1, -1, -1))
     for dd in range(2):
         for l in range(layers):
+            if dd == 1 and l == layers - 1:
+                take_raw(0)
+                emit(True, 0, ks)
             if dd == 0:
                 basis_copy(l).wait()
             own_copy(l, dd).wait()
@@ -211,7 +246,12 @@
                 basis_buf[l], x_buf[dd, l], (((0,), (0,)), ((), ())),
                 preferred_element_type=jnp.float32,
             ).astype(jnp.bfloat16)
-            coeff_buf[l] = coeff
+            coeff_buf[dd, l] = coeff
+
+            @pl.when(inner)
+            def _():
+                raw_copy(dd, l).start()
+
             gram = lax.dot_general(
                 coeff, coeff, (((1,), (1,)), ((), ())), preferred_element_type=jnp.float32
             )
@@ -254,15 +294,16 @@
         def _():
             pltpu.make_async_copy(slot_mine, slot_buf.at[dd], slot_own).wait()
 
+        @pl.when(inner)
+        def _():
+            raw_slot_copy(dd).start()
+
         if dd == 0:
-            emit(0, range(REACH - 1, -1, -1))
-
-    ks = list(range(REACH - 1, -1, -1))
-    emit(1, ks[:2])
+            emit(False, 0, ks)
+
     pair_copy().wait()
     part_buf[half_of(core), :] += pair_buf[...]
     loop(1, chips, lambda r: rs_copy(r).start())
-    emit(1, ks[2:4])
     loop(1, chips, lambda r: rs_copy(r).wait())
     total = part_buf[rows_of(chip), :]
     for r in range(1, chips):
@@ -270,12 +311,15 @@
     full_buf[side, rows_of(chip), :] = total
     mirror_copy().start()
     loop(1, chips, lambda r: ag_copy(r).start())
-    emit(1, ks[4:6])
+    emit(False, 1, ks[:4])
+    emit(False, 1, ks[4:])
     loop(1, chips, lambda r: ag_copy(r).wait_recv())
     sib_copy(side).start()
     mirror_copy().wait_recv()
     loop(1, chips, lambda r: fwd_copy(r).start())
-    emit(1, ks[6:])
+    take_raw(1)
+    emit(True, 1, ks[:4])
+    emit(True, 1, ks[4:])
     loop(1, chips, lambda r: fwd_copy(r).wait_recv())
     sib_copy(1 - side).start()
     sib_copy(0).wait()
@@ -307,27 +351,37 @@
     for dd in range(2):
         for l in range(layers):
             loop(1, m, lambda r: x_copy(l, dd, r).wait_send())
-        for k in range(REACH):
-            to = lax.rem(held(q, dd) + k, n)
-
-            @pl.when(to != me)
-            def _():
-                out_copy(dd, k).wait_send()
-
-            @pl.when(to == me)
-            def _():
-                out_local(dd, k).wait()
+        @pl.when(inner)
+        def _():
+            for l in range(layers):
+                raw_copy(dd, l).wait_send()
+            raw_slot_copy(dd).wait_send()
+
+        for relay in (False, True):
+            for k in range(REACH):
+                sent = is_sent(relay, dd, k)
+                away = owner(relay, dd, k) != me
+
+                @pl.when(jnp.logical_and(sent, away))
+                def _():
+                    out_copy(relay, dd, k).wait_send()
+
+                @pl.when(jnp.logical_and(sent, jnp.logical_not(away)))
+                def _():
+                    out_local(relay, dd, k).wait()
 
     for hh in range(2):
         for k in range(REACH):
-            sender = hh * m + holder(lax.rem(me - k + n, n))
+            held_by = holder(lax.rem(me - k + n, n))
+            relayed = jnp.logical_and(side != hh, held_by // (m // 2) == 1 - hh)
+            sender = hh * m + held_by + jnp.where(relayed, (1 - 2 * hh) * (m // 2), 0)
 
             @pl.when(sender != me)
             def _():
                 at = recv_ref.at[
                     pl.ds(OWNER_SLOT_LIMIT * k, OWNER_SLOT_LIMIT), pl.ds(hh * rank, rank), :
                 ]
-                remote(at, at, out_send.at[0, 0], out_recv.at[hh, k], me).wait_recv()
+                remote(at, at, out_send.at[0, 0, 0], out_recv.at[hh, k], me).wait_recv()
 
 
 def per_device(key_values, bases, owner_slots):
@@ -356,9 +410,11 @@
         scratch_shapes=[
             vmem((2, layers, width, span), jnp.bfloat16),
             vmem((layers, width, rank), jnp.bfloat16),
-            vmem((layers, rank, span), jnp.bfloat16),
-            vmem((2, CAP, rank, unit), jnp.bfloat16),
+            vmem((2, layers, rank, span), jnp.bfloat16),
+            vmem((2, layers, rank, span), jnp.bfloat16),
+            vmem((2, 2, CAP, rank, unit), jnp.bfloat16),
             vmem((8, LANES), jnp.int32),
+            vmem((2, 8, LANES), jnp.int32),
             vmem((2, 8, LANES), jnp.int32),
             vmem((m * piece, LANES), jnp.float32),
             vmem((chips * piece, LANES), jnp.float32),
@@ -368,7 +424,8 @@
             dma((2,)), dma((2,)), dma,
             dma, dma, dma((chips,)), dma((chips,)), dma((chips,)), dma((chips,)), dma, dma,
             dma((chips,)), dma((chips,)),
-            dma((2,)), dma((2,)), dma((2, REACH)), dma((2, REACH)), dma((2,)),
+            dma((2,)), dma((2,)), dma((2, layers)), dma((2, layers)), dma((2,)), dma((2,)),
+            dma((2, 2, REACH)), dma((2, REACH)), dma((2, 2)),
         ],
         compiler_params=pltpu.CompilerParams(
             collective_id=0, has_side_effects=True, vmem_limit_bytes=58 * 1024 * 1024

time: 108 us -> 105 us (0.972)
  the two profiles are of different devices: /device:TPU:1 before, /device:TPU:19 now
where the time goes in v3:
time: 105 us
  Pallas kernels  97.6 us (93%)
  local copies, waits for them, and re-layouts  6.32 us (6%)
    pallas_call x1, Pallas kernels, per_device(): pl.pallas_call(functools.partial(kernel, n, layers, width, rank, span, pi...  97.6 us
    unnamed x8, local copies, waits for them, and re-layouts  6.32 us

profile of v3, /device:TPU:19, one launch (start us, length us, event | category | flops | bytes accessed | tf_op | source)
XLA Modules:
  0.0 104.5 jit_solution(7932812184329134774)
XLA Ops:
  0.6 1.3 %copy.6.slot_ref = s32[3,2]{1,0:T(4,128)} copy(s32[3,2]{0,1:T(2,128)} %param.5) | data formatting | bytes 48 | tf_op args[2]
  2.0 97.6 %compress_handoff.1 = (bf16[16,512,128]{2,1,0:T(8,128)(2,1)}, f32[3,2,256,256]{3,2,1,0:T(8,128)}, f32[3,2,1024]{2,1,0:T(2,128)}) custom-call(bf16[3,128,4096]{2,1,0:T(8,128)(2,1)} %kv_ref.1, bf16[3,2,1024,256]{3,2,1,0:T(8,128)(2,1)} %bases_ref.1, s32[3,2]{1,0:T(4,128)} %copy.6.slot_ref), custom_call_target="tpu_custom_call" | custom-call | tf_op jit(solution)/shard_map/compress_handoff/pallas_call | solution.py:401
  99.5 0.0 copy-start
  99.5 3.2 %copy.10 = bf16[16,512,128]{2,1,0:T(8,128)(2,1)} copy(bf16[16,512,128]{2,1,0:T(8,128)(2,1)} %get-tuple-element.6) | data formatting | bytes 4194304
  102.8 0.0 copy-done
  102.8 0.0 copy-start.1
  102.8 1.1 %copy.11 = f32[3,2,256,256]{3,2,1,0:T(8,128)} copy(f32[3,2,256,256]{3,2,1,0:T(8,128)S(1)} %copy-done) | data formatting | bytes 3145728
  103.9 0.0 copy-done.1
  103.9 0.6 copy.12
Async XLA Ops:
  99.5 3.2 %copy-start = (f32[3,2,256,256]{3,2,1,0:T(8,128)S(1)}, f32[3,2,256,256]{3,2,1,0:T(8,128)}, u32[]{:S(2)}) copy-start(f32[3,2,256,256]{3,2,1,0:T(8,128)} %get-tuple-element.7) | copy-start | bytes 4718596
  102.8 1.1 %copy-start.1 = (f32[3,2,1024]{2,1,0:T(2,128)S(1)}, f32[3,2,1024]{2,1,0:T(2,128)}, u32[]{:S(2)}) copy-start(f32[3,2,1024]{2,1,0:T(2,128)} %get-tuple-element.8) | copy-start | bytes 73732
